TPU v7x, 32 devices: a whole 2x2x4 slice. The times are simulated.
32 devices in a mesh: dp: 8 (over y, x, core), ffn: 4 (over z).
Axes of the slice: x: 2, y: 2, z: 4, core: 2. Of those that a mesh axis runs over, the one named last changes fastest.
Arguments:
- seg_input: bfloat16 [2, 8, 512, 1024], P(None, 'dp', 'ffn'), may hold values from -6 to 6
- memory: bfloat16 [2, 8, 384, 1024], P(None, 'dp', 'ffn'), may hold values from -6 to 6
- compressed: bfloat16 [2, 8, 512, 1024], P(None, 'dp', 'ffn'), may hold values from -6 to 6
- mem_fill: int32 [2, 8], P(None, 'dp'), may hold values from 0 to 384, as said below
- comp_fill: int32 [2, 8], P(None, 'dp'), may hold values from 0 to 512, as said below
- attn_gain: float32 [1024], replicated, may hold values from 0.5 to 1.5
- attn_shift: float32 [1024], replicated, may hold values from -1.75 to 1.75
- attn_weights: bfloat16 [4096, 1024], replicated, may hold values from -1.5 to 1.5
- rel_table: float32 [8, 22], replicated, may hold values from -6 to 6
- ffn_gain: float32 [1024], replicated, may hold values from 0.5 to 1.5
- ffn_shift: float32 [1024], replicated, may hold values from -1.75 to 1.75
- w_up: bfloat16 [1024, 4096], P(None, 'ffn'), may hold values from -0.1875 to 0.1875
- b_up: float32 [4096], P('ffn'), may hold values from -1.75 to 1.75
- w_down: bfloat16 [4096, 1024], P('ffn'), may hold values from -0.125 to 0.125
- b_down: float32 [1024], replicated, may hold values from -1.75 to 1.75
- conv_weight: bfloat16 [3072, 1024], replicated, may hold values from -0.109375 to 0.109375
- conv_bias: float32 [1024], replicated, may hold values from -1.75 to 1.75
- out_grad: bfloat16 [2, 8, 512, 1024], P(None, 'dp', 'ffn'), may hold values from -6 to 6
- comp_grad: bfloat16 [2, 8, 128, 1024], P(None, 'dp', 'ffn'), may hold values from -6 to 6
Outputs:
- layer_out: bfloat16 [2, 8, 512, 1024], P(None, 'dp', 'ffn')
- new_compressed: bfloat16 [2, 8, 128, 1024], P(None, 'dp', 'ffn')
- seg_grad: float32 [2, 8, 512, 1024], P(None, 'dp', 'ffn')
- attn_gain_grad: float32 [1024], replicated
- attn_shift_grad: float32 [1024], replicated
- attn_weights_grad: float32 [4096, 1024], P(('dp', 'ffn'))
- rel_table_grad: float32 [8, 22], replicated
- ffn_gain_grad: float32 [1024], replicated
- ffn_shift_grad: float32 [1024], replicated
- w_up_grad: float32 [1024, 4096], P('dp', 'ffn')
- b_up_grad: float32 [4096], replicated
- w_down_grad: float32 [4096, 1024], P('ffn', 'dp')
- b_down_grad: float32 [1024], replicated
- conv_weight_grad: float32 [3072, 1024], replicated
- conv_bias_grad: float32 [1024], replicated
Inputs may be any that keep to these rules, and one draw needn't show every extreme that they name: `mem_fill`: in every micro-batch one stream has all 384 memory slots live and another none; live slots are the newest, at the end of the buffer. `comp_fill`: in every micro-batch one stream has all 512 compressed slots live and another none; live slots are the newest, at the end of the buffer.
All inputs are finite; a program needn't handle non-finite values.
Results may differ from a plain program's by a relative error of at most 0.028.
Values may be sent and summed in bfloat16 or wider, within the bound.
No kernel may reach another device: no remote copies, remote signals or barrier semaphores. Data moves between devices by JAX's collectives and lax.ppermute only.
A program may use at most 320 MiB of HBM per device.

v0:
```python
import jax
import jax.numpy as jnp
from jax import lax
from jax.sharding import PartitionSpec as P

D = 1024
H = 8
HD = 128
M = 384
CM = 512
PW = 64
KR = 1408
NB = 22


EPSILON = 1e-05
MASKED_SCORE = -1e30


def normalize(rows_in, gain, shift):
    centre = jnp.mean(rows_in, axis=-1, keepdims=True)
    centred = rows_in - centre
    variance = jnp.mean(centred * centred, axis=-1, keepdims=True)
    return centred * lax.rsqrt(variance + EPSILON) * gain + shift


def smooth_unit(values_in):
    return jax.nn.gelu(values_in, approximate=False)


def matmul(left, right):
    return jnp.dot(left, right, preferred_element_type=jnp.float32)


def contract_rows(left, right):
    return lax.dot_general(
        left, right, (((0,), (0,)), ((), ())), preferred_element_type=jnp.float32
    )


def times_transposed(left, right):
    return lax.dot_general(
        left, right, (((1,), (1,)), ((), ())), preferred_element_type=jnp.float32
    )


def norm_backward(rows_in, gain, shift, cotangent):
    outputs, pullback = jax.vjp(normalize, rows_in, gain, shift)
    return pullback(cotangent)


def on_device(
    seg_input,
    memory,
    compressed,
    mem_fill,
    comp_fill,
    attn_gain,
    attn_shift,
    attn_weights,
    rel_table,
    ffn_gain,
    ffn_shift,
    w_up,
    b_up,
    w_down,
    b_down,
    conv_weight,
    conv_bias,
    out_grad,
    comp_grad,
):
    groups = lax.axis_size("ffn")
    ffn_rank = lax.axis_index("ffn")
    seg_rows = seg_input.shape[2]
    mem_rows = memory.shape[2]
    hidden_local = w_up.shape[1]
    query_tiles = seg_rows // PW
    score_scale = HD ** (-0.5)
    w_query = attn_weights[:D]
    w_key = attn_weights[D : 2 * D]
    w_value = attn_weights[2 * D : 3 * D]
    w_out = attn_weights[3 * D :]
    key_pos = jnp.arange(KR, dtype=jnp.int32)
    query_pos = CM + M + ffn_rank * seg_rows + jnp.arange(seg_rows, dtype=jnp.int32)
    query_blocks = (
        (CM + M) // PW + ffn_rank * query_tiles + jnp.arange(query_tiles, dtype=jnp.int32)
    )
    distance = query_blocks[:, None] - jnp.arange(NB, dtype=jnp.int32)[None, :]
    one_hot = (distance[:, :, None] == jnp.arange(NB, dtype=jnp.int32)[None, None, :]).astype(
        jnp.float32
    )
    tile_bias = jnp.einsum("hn,qkn->hqk", rel_table, one_hot, precision=lax.Precision.HIGHEST)
    memory_pos = ffn_rank * mem_rows + jnp.arange(mem_rows, dtype=jnp.int32)

    def scores_of(queries, key_heads, key_mask):
        raw_scores = (
            jnp.einsum("qhd,khd->hqk", queries, key_heads, preferred_element_type=jnp.float32)
            * score_scale
        )
        tiled = raw_scores.reshape(H, query_tiles, PW, NB, PW) + tile_bias[:, :, None, :, None]
        return jnp.where(key_mask[None], tiled.reshape(H, seg_rows, KR), MASKED_SCORE)

    def micro_batch(totals, sample):
        segment, memory_now, compressed_now, mem_count, comp_count, grad_rows_in, comp_cot = sample
        segment_f = segment.astype(jnp.float32)
        sources = (compressed_now.astype(jnp.float32), memory_now.astype(jnp.float32), segment_f)
        lowered = [
            normalize(section, attn_gain, attn_shift).astype(jnp.bfloat16) for section in sources
        ]
        own_keys = [matmul(section, w_key).astype(jnp.bfloat16) for section in lowered]
        own_values = [matmul(section, w_value).astype(jnp.bfloat16) for section in lowered]
        gathered = (
            lax.all_gather(own_keys[0], "ffn", axis=0, tiled=True),
            lax.all_gather(own_keys[1], "ffn", axis=0, tiled=True),
            lax.all_gather(own_keys[2], "ffn", axis=0, tiled=True),
            lax.all_gather(own_values[0], "ffn", axis=0, tiled=True),
            lax.all_gather(own_values[1], "ffn", axis=0, tiled=True),
            lax.all_gather(own_values[2], "ffn", axis=0, tiled=True),
        )
        key_heads = jnp.concatenate(gathered[:3], axis=0).reshape(KR, H, HD)
        value_heads = jnp.concatenate(gathered[3:], axis=0).reshape(KR, H, HD)
        queries = matmul(lowered[2], w_query).astype(jnp.bfloat16).reshape(seg_rows, H, HD)
        live_keys = jnp.where(
            key_pos < CM,
            key_pos >= CM - comp_count,
            jnp.where(key_pos < CM + M, key_pos >= CM + M - mem_count, True),
        )
        key_mask = live_keys[None, :] & (key_pos[None, :] <= query_pos[:, None])
        scores = scores_of(queries, key_heads, key_mask)
        row_max = jnp.max(scores, axis=-1, keepdims=True)
        expanded = jnp.exp(scores - row_max)
        row_total = jnp.sum(expanded, axis=-1, keepdims=True)
        log_total = row_max + jnp.log(row_total)
        attention = (expanded / row_total).astype(jnp.bfloat16)
        mixed_heads = jnp.einsum(
            "hqk,khd->qhd", attention, value_heads, preferred_element_type=jnp.float32
        )
        mixed_heads = mixed_heads.reshape(seg_rows, D).astype(jnp.bfloat16)
        residual = segment_f + matmul(mixed_heads, w_out)
        ffn_in = normalize(residual, ffn_gain, ffn_shift).astype(jnp.bfloat16)
        ffn_rows = lax.all_gather(ffn_in, "ffn", axis=0, tiled=True)
        hidden_pre = matmul(ffn_rows, w_up) + b_up
        activated_f, smooth_pull = jax.vjp(smooth_unit, hidden_pre)
        activated = activated_f.astype(jnp.bfloat16)
        branch = lax.psum_scatter(
            matmul(activated, w_down).astype(jnp.bfloat16), "ffn", scatter_dimension=0, tiled=True
        ).astype(jnp.float32)
        layer_rows = (residual + branch + b_down).astype(jnp.bfloat16)
        alive_rows = memory_pos >= M - mem_count
        flat_memory = jnp.where(
            alive_rows[:, None], memory_now, jnp.zeros_like(memory_now)
        ).reshape(mem_rows // 3, 3 * D)
        compressed_new = (matmul(flat_memory, conv_weight) + conv_bias).astype(jnp.bfloat16)
        grad_out = grad_rows_in.astype(jnp.float32)
        grad_all = lax.all_gather(grad_rows_in, "ffn", axis=0, tiled=True)
        grad_hidden = times_transposed(grad_all, w_down)
        grad_pre = smooth_pull(grad_hidden)[0].astype(jnp.bfloat16)
        down_grad = contract_rows(activated, grad_all)
        up_grad = contract_rows(ffn_rows, grad_pre)
        up_bias_part = jnp.sum(grad_pre.astype(jnp.float32), axis=0)
        grad_ffn_in = lax.psum_scatter(
            times_transposed(grad_pre, w_up).astype(jnp.bfloat16),
            "ffn",
            scatter_dimension=0,
            tiled=True,
        ).astype(jnp.float32)
        grad_normal, ffn_gain_part, ffn_shift_part = norm_backward(
            residual, ffn_gain, ffn_shift, grad_ffn_in
        )
        grad_residual = grad_out + grad_normal
        grad_branch = grad_residual.astype(jnp.bfloat16)
        out_weight_grad = contract_rows(mixed_heads, grad_branch)
        grad_mixed = (
            times_transposed(grad_branch, w_out).astype(jnp.bfloat16).reshape(seg_rows, H, HD)
        )
        scores_again = scores_of(queries, key_heads, key_mask)
        attention_f = jnp.exp(scores_again - log_total)
        grad_attention = jnp.einsum(
            "qhd,khd->hqk", grad_mixed, value_heads, preferred_element_type=jnp.float32
        )
        row_inner = jnp.sum(attention_f * grad_attention, axis=-1, keepdims=True)
        grad_scores = (attention_f * (grad_attention - row_inner)).astype(jnp.bfloat16)
        tile_grad = jnp.sum(
            grad_scores.astype(jnp.float32).reshape(H, query_tiles, PW, NB, PW), axis=(2, 4)
        )
        table_grad = jnp.einsum("hqk,qkn->hn", tile_grad, one_hot, precision=lax.Precision.HIGHEST)
        grad_query = (
            jnp.einsum("hqk,khd->qhd", grad_scores, key_heads, preferred_element_type=jnp.float32)
            * score_scale
        )
        grad_query = grad_query.reshape(seg_rows, D).astype(jnp.bfloat16)
        key_part = (
            jnp.einsum(
                "hqk,qhd->khd", grad_scores, queries, preferred_element_type=jnp.float32
            ).reshape(KR, D)
            * score_scale
        )
        value_part = jnp.einsum(
            "hqk,qhd->khd",
            attention_f.astype(jnp.bfloat16),
            grad_mixed,
            preferred_element_type=jnp.float32,
        ).reshape(KR, D)
        own_grads = (
            lax.psum_scatter(
                key_part[:CM].astype(jnp.bfloat16), "ffn", scatter_dimension=0, tiled=True
            ).astype(jnp.float32),
            lax.psum_scatter(
                key_part[CM : CM + M].astype(jnp.bfloat16), "ffn", scatter_dimension=0, tiled=True
            ).astype(jnp.float32),
            lax.psum_scatter(
                key_part[CM + M :].astype(jnp.bfloat16), "ffn", scatter_dimension=0, tiled=True
            ).astype(jnp.float32),
            lax.psum_scatter(
                value_part[:CM].astype(jnp.bfloat16), "ffn", scatter_dimension=0, tiled=True
            ).astype(jnp.float32),
            lax.psum_scatter(
                value_part[CM : CM + M].astype(jnp.bfloat16), "ffn", scatter_dimension=0, tiled=True
            ).astype(jnp.float32),
            lax.psum_scatter(
                value_part[CM + M :].astype(jnp.bfloat16), "ffn", scatter_dimension=0, tiled=True
            ).astype(jnp.float32),
        )
        grad_keys = [section.astype(jnp.bfloat16) for section in own_grads[:3]]
        grad_values = [section.astype(jnp.bfloat16) for section in own_grads[3:]]
        grad_normed = [
            times_transposed(grad_keys[section_id], w_key)
            + times_transposed(grad_values[section_id], w_value)
            for section_id in range(3)
        ]
        grad_normed[2] = grad_normed[2] + times_transposed(grad_query, w_query)
        query_weight_grad = contract_rows(lowered[2], grad_query)
        key_weight_grad = (
            contract_rows(lowered[0], grad_keys[0])
            + contract_rows(lowered[1], grad_keys[1])
            + contract_rows(lowered[2], grad_keys[2])
        )
        value_weight_grad = (
            contract_rows(lowered[0], grad_values[0])
            + contract_rows(lowered[1], grad_values[1])
            + contract_rows(lowered[2], grad_values[2])
        )
        norm_parts = [
            norm_backward(sources[section_id], attn_gain, attn_shift, grad_normed[section_id])
            for section_id in range(3)
        ]
        grad_segment = grad_residual + norm_parts[2][0]
        attn_gain_part = norm_parts[0][1] + norm_parts[1][1] + norm_parts[2][1]
        attn_shift_part = norm_parts[0][2] + norm_parts[1][2] + norm_parts[2][2]
        conv_grad = contract_rows(flat_memory, comp_cot)
        conv_bias_part = jnp.sum(comp_cot.astype(jnp.float32), axis=0)
        down_bias_part = jnp.sum(grad_out, axis=0)
        updates = (
            attn_gain_part,
            attn_shift_part,
            query_weight_grad,
            key_weight_grad,
            value_weight_grad,
            out_weight_grad,
            table_grad,
            ffn_gain_part,
            ffn_shift_part,
            up_grad,
            up_bias_part,
            down_grad,
            down_bias_part,
            conv_grad,
            conv_bias_part,
        )
        totals = jax.tree.map(jnp.add, totals, updates)
        return (totals, (layer_rows, compressed_new, grad_segment))

    float_zero = jnp.float32
    zero_grads = (
        jnp.zeros((D,), float_zero),
        jnp.zeros((D,), float_zero),
        jnp.zeros((D, D), float_zero),
        jnp.zeros((D, D), float_zero),
        jnp.zeros((D, D), float_zero),
        jnp.zeros((D, D), float_zero),
        jnp.zeros(rel_table.shape, float_zero),
        jnp.zeros((D,), float_zero),
        jnp.zeros((D,), float_zero),
        jnp.zeros(w_up.shape, float_zero),
        jnp.zeros((hidden_local,), float_zero),
        jnp.zeros(w_down.shape, float_zero),
        jnp.zeros((D,), float_zero),
        jnp.zeros(conv_weight.shape, float_zero),
        jnp.zeros((D,), float_zero),
    )
    samples = (
        seg_input[:, 0],
        memory[:, 0],
        compressed[:, 0],
        mem_fill[:, 0],
        comp_fill[:, 0],
        out_grad[:, 0],
        comp_grad[:, 0],
    )
    totals, stacked = lax.scan(micro_batch, zero_grads, samples)
    attn_grad = jnp.concatenate([totals[2], totals[3], totals[4], totals[5]], axis=0)
    attn_grad = lax.psum_scatter(attn_grad, ("dp", "ffn"), scatter_dimension=0, tiled=True)
    up_weight_grad, down_weight_grad = (
        lax.psum_scatter(totals[9], "dp", scatter_dimension=0, tiled=True),
        lax.psum_scatter(totals[11], "dp", scatter_dimension=1, tiled=True),
    )
    up_bias_full = lax.dynamic_update_slice(
        jnp.zeros((hidden_local * groups,), jnp.float32), totals[10], (ffn_rank * hidden_local,)
    )
    shared = lax.psum(
        (
            totals[13],
            totals[14],
            totals[0],
            totals[1],
            totals[7],
            totals[8],
            totals[12],
            totals[6],
            up_bias_full,
        ),
        ("dp", "ffn"),
    )
    return (
        stacked[0][:, None],
        stacked[1][:, None],
        stacked[2][:, None],
        shared[2],
        shared[3],
        attn_grad,
        shared[7],
        shared[4],
        shared[5],
        up_weight_grad,
        shared[8],
        down_weight_grad,
        shared[6],
        shared[0],
        shared[1],
    )


def solution(mesh):
    return jax.shard_map(
        on_device,
        mesh=mesh,
        in_specs=(
            P(None, "dp", "ffn", None),
            P(None, "dp", "ffn", None),
            P(None, "dp", "ffn", None),
            P(None, "dp"),
            P(None, "dp"),
            P(),
            P(),
            P(),
            P(),
            P(),
            P(),
            P(None, "ffn"),
            P("ffn"),
            P("ffn", None),
            P(),
            P(),
            P(),
            P(None, "dp", "ffn", None),
            P(None, "dp", "ffn", None),
        ),
        out_specs=(
            P(None, "dp", "ffn", None),
            P(None, "dp", "ffn", None),
            P(None, "dp", "ffn", None),
            P(),
            P(),
            P(("dp", "ffn"), None),
            P(),
            P(),
            P(),
            P("dp", "ffn"),
            P(),
            P("ffn", "dp"),
            P(),
            P(),
            P(),
        ),
        check_vma=False,
    )
```

profile of v0, /device:TPU:0, one launch (start us, length us, event | category | flops | bytes accessed | tf_op | source)
XLA Modules:
  0.0 1478.5 jit_solution(13740428444911833908)
XLA Ops:
  9.4 5.8 fusion.130
  15.3 883.1 %while.46 = (s32[]{:T(128)}, f32[1024]{0:T(1024)}, f32[1024]{0:T(1024)}, f32[1024,1024]{1,0:T(8,128)}, f32[1024,1024]{1,0:T(8,128)}, /*index=5*/f32[1024,1024]{1...) while((s32[]{:T(128)}, f32[1024]{0:T(1024)}, ...), condition=%wide.region_36.37_spmd.clone.clone, body=%wide.region_0.36_spmd.clone.clone.sunk | while | flops 15250011136 | bytes 700114752 | solution.py:301
  27.4 31.8 %all_gather.47 = bf16[384,1024]{1,0:T(8,128)(2,1)} all-gather(bf16[96,1024]{1,0:T(8,128)(2,1)S(1)} %convolution_convert_fusion.23), channel_id=1, replica_groups=mesh['dp'=8,'ffn'=4] {'ffn'}, dimensions={0}, use_global_device_ids=true | all-gather | bytes 983040 | tf_op jit(solution)/shard_map/while/body/eval_jaxpr/all_gather | solution.py:115
  67.7 11.6 add.700
  79.4 6.3 copy.115
  87.1 21.6 %all_gather.50 = bf16[384,1024]{1,0:T(8,128)(2,1)} all-gather(bf16[96,1024]{1,0:T(8,128)(2,1)S(1)} %convolution_convert_fusion.26), channel_id=1, replica_groups=mesh['dp'=8,'ffn'=4] {'ffn'}, dimensions={0}, use_global_device_ids=true | all-gather | bytes 983040 | tf_op jit(solution)/shard_map/while/body/eval_jaxpr/all_gather | solution.py:118
  116.9 5.1 fusion.378
  125.5 26.3 %all-gather.17.cloned.1.call-done = bf16[512,1024]{1,0:T(8,128)(2,1)} async-done(((bf16[128,1024]{1,0:T(8,128)(2,1)}), bf16[512,1024]{1,0:T(8,128)(2,1)}) %all-gather.17.cloned.1.call-update) | async-done | bytes 1048592 | tf_op jit(solution)/shard_map/while/body/eval_jaxpr/all_gather | solution.py:117
  151.8 5.4 fusion.380
  162.0 24.7 %all-gather.19.cloned.1.call-done = bf16[512,1024]{1,0:T(8,128)(2,1)} async-done(((bf16[128,1024]{1,0:T(8,128)(2,1)}), bf16[512,1024]{1,0:T(8,128)(2,1)}) %all-gather.19.cloned.1.call-update) | async-done | bytes 1048592 | tf_op jit(solution)/shard_map/while/body/eval_jaxpr/all_gather | solution.py:142
  186.6 8.7 multiply_convert_fusion.5
  195.3 20.8 %all-gather.21.cloned.1.call-done = bf16[1,512,1024]{2,1,0:T(8,128)(2,1)} async-done(((bf16[1,128,1024]{2,1,0:T(8,128)(2,1)}), bf16[1,512,1024]{2,1,0:T(8,128)(2,1)}) %all-gather.21.cloned.1.call-update) | async-done | bytes 1048592 | tf_op jit(solution)/shard_map/while/body/eval_jaxpr/all_gather | solution.py:156
  216.1 5.8 convert_reduce_fusion.17
  229.5 22.5 %reduce-scatter.42.cloned.1.call-done = bf16[128,1024]{1,0:T(8,128)(2,1)} async-done(((bf16[512,1024]{1,0:T(8,128)(2,1)}), bf16[128,1024]{1,0:T(8,128)(2,1)}) %reduce-scatter.42.cloned.1.call-update) | async-done | bytes 262160 | tf_op jit(solution)/shard_map/while/body/eval_jaxpr/reduce_scatter | solution.py:162
  261.2 5.6 multiply_reduce_fusion.5
  303.8 6.6 select_add_fusion.35
  321.3 5.2 copy.124
  328.8 11.9 reshape.355
  340.6 10.8 reduce_sum.432
  376.0 10.2 reduce-scatter.46.cloned.1.call-done
  392.3 21.9 %reduce-scatter.48.cloned.1.call-done = bf16[128,1024]{1,0:T(8,128)(2,1)} async-done(((bf16[512,1024]{1,0:T(8,128)(2,1)}), bf16[128,1024]{1,0:T(8,128)(2,1)}) %reduce-scatter.48.cloned.1.call-update) | async-done | bytes 262160 | tf_op jit(solution)/shard_map/while
  416.8 25.5 %reduce-scatter.50.cloned.1.call-done = bf16[128,1024]{1,0:T(8,128)(2,1)} async-done(((bf16[512,1024]{1,0:T(8,128)(2,1)}), bf16[128,1024]{1,0:T(8,128)(2,1)}) %reduce-scatter.50.cloned.1.call-update) | async-done | bytes 262160 | tf_op jit(solution)/shard_map/while
  469.6 30.1 %all_gather.47 = bf16[384,1024]{1,0:T(8,128)(2,1)} all-gather(bf16[96,1024]{1,0:T(8,128)(2,1)S(1)} %convolution_convert_fusion.23), channel_id=1, replica_groups=mesh['dp'=8,'ffn'=4] {'ffn'}, dimensions={0}, use_global_device_ids=true | all-gather | bytes 983040 | tf_op jit(solution)/shard_map/while/body/eval_jaxpr/all_gather | solution.py:115
  508.3 11.7 add.700
  520.0 6.2 copy.115
  527.7 20.5 %all_gather.50 = bf16[384,1024]{1,0:T(8,128)(2,1)} all-gather(bf16[96,1024]{1,0:T(8,128)(2,1)S(1)} %convolution_convert_fusion.26), channel_id=1, replica_groups=mesh['dp'=8,'ffn'=4] {'ffn'}, dimensions={0}, use_global_device_ids=true | all-gather | bytes 983040 | tf_op jit(solution)/shard_map/while/body/eval_jaxpr/all_gather | solution.py:118
  556.5 5.1 fusion.378
  565.1 24.6 %all-gather.17.cloned.1.call-done = bf16[512,1024]{1,0:T(8,128)(2,1)} async-done(((bf16[128,1024]{1,0:T(8,128)(2,1)}), bf16[512,1024]{1,0:T(8,128)(2,1)}) %all-gather.17.cloned.1.call-update) | async-done | bytes 1048592 | tf_op jit(solution)/shard_map/while/body/eval_jaxpr/all_gather | solution.py:117
  589.7 5.4 fusion.380
  599.6 25.0 %all-gather.19.cloned.1.call-done = bf16[512,1024]{1,0:T(8,128)(2,1)} async-done(((bf16[128,1024]{1,0:T(8,128)(2,1)}), bf16[512,1024]{1,0:T(8,128)(2,1)}) %all-gather.19.cloned.1.call-update) | async-done | bytes 1048592 | tf_op jit(solution)/shard_map/while/body/eval_jaxpr/all_gather | solution.py:142
  624.6 8.7 multiply_convert_fusion.5
  633.3 20.8 %all-gather.21.cloned.1.call-done = bf16[1,512,1024]{2,1,0:T(8,128)(2,1)} async-done(((bf16[1,128,1024]{2,1,0:T(8,128)(2,1)}), bf16[1,512,1024]{2,1,0:T(8,128)(2,1)}) %all-gather.21.cloned.1.call-update) | async-done | bytes 1048592 | tf_op jit(solution)/shard_map/while/body/eval_jaxpr/all_gather | solution.py:156
  654.0 5.8 convert_reduce_fusion.17
  667.5 22.5 %reduce-scatter.42.cloned.1.call-done = bf16[128,1024]{1,0:T(8,128)(2,1)} async-done(((bf16[512,1024]{1,0:T(8,128)(2,1)}), bf16[128,1024]{1,0:T(8,128)(2,1)}) %reduce-scatter.42.cloned.1.call-update) | async-done | bytes 262160 | tf_op jit(solution)/shard_map/while/body/eval_jaxpr/reduce_scatter | solution.py:162
  699.1 5.6 multiply_reduce_fusion.5
  741.8 11.2 select_add_fusion.35
  755.5 6.2 select_add_fusion.31
  761.8 5.6 select_add_fusion.33
  767.4 5.2 copy.124
  774.8 11.9 reshape.355
  786.7 11.0 reduce_sum.432
  832.0 20.0 %reduce-scatter.48.cloned.1.call-done = bf16[128,1024]{1,0:T(8,128)(2,1)} async-done(((bf16[512,1024]{1,0:T(8,128)(2,1)}), bf16[128,1024]{1,0:T(8,128)(2,1)}) %reduce-scatter.48.cloned.1.call-update) | async-done | bytes 262160 | tf_op jit(solution)/shard_map/while
  854.6 25.6 %reduce-scatter.50.cloned.1.call-done = bf16[128,1024]{1,0:T(8,128)(2,1)} async-done(((bf16[512,1024]{1,0:T(8,128)(2,1)}), bf16[128,1024]{1,0:T(8,128)(2,1)}) %reduce-scatter.50.cloned.1.call-update) | async-done | bytes 262160 | tf_op jit(solution)/shard_map/while
  900.4 12.7 pad_maximum_fusion.1
  914.0 40.7 %all-reduce = (f32[1024]{0:T(1024)}, f32[1024]{0:T(1024)}, f32[8,22]{1,0:T(8,128)}, f32[1024]{0:T(1024)}, f32[1024]{0:T(1024)}, /*index=5*/f32[4096]{0:T(1024)}, f32[1024]{0:T(1024)}, f32[1024]{0:T(1024)}) all-reduce(f32[1024]{0:T(1024)S(1)} %copy-done.75, f32[1024]{0:T(1024)S(1)} %copy-done.78, ...), channel_id=1, replica_groups=mesh['dp'=8,'ffn'=4] {'dp','ffn'}, use_global_device_ids=true, to_apply=%region_37.38 | all-reduce | flops 10416 | bytes 83328 | tf_op jit(solution)/shard_map/psum | solution.py:311
  954.7 400.0 %all-reduce.3.cloned.1.call-done = f32[3072,1024]{1,0:T(8,128)} async-done(((f32[3072,1024]{1,0:T(8,128)}), f32[3072,1024]{1,0:T(8,128)}) %all-reduce.3.cloned.1.call-update) | async-done | bytes 12582928 | tf_op jit(solution)/shard_map/psum | solution.py:311
  1354.7 104.0 %reduce-scatter.36.cloned.1.call-done = f32[128,1024]{1,0:T(8,128)} async-done(((f32[4096,1024]{1,0:T(8,128)}), f32[128,1024]{1,0:T(8,128)}) %reduce-scatter.36.cloned.1.call-update) | async-done | bytes 524304 | tf_op jit(solution)/shard_map/reduce_scatter | solution.py:303
  1458.7 12.1 copy.190
  (669 shorter events, 299.8 us)
Async XLA Ops:
  15.5 47.3 %copy-start.41 = (f32[8,2,22]{1,2,0:T(8,128)}, f32[8,2,22]{1,2,0:T(8,128)S(1)}, u32[]{:S(2)}) copy-start(f32[8,2,22]{1,2,0:T(8,128)S(1)} %get-tuple-element.1274) | copy-start | bytes 4228 | tf_op jit(solution)/shard_map/while
  15.5 93.1 %all-gather.11.cloned.1.call-start = ((), (), s32[]{:S(2)}) async-start(), calls=%async_computation.15 | async-start | bytes 1310720 | tf_op jit(solution)/shard_map/while/body/eval_jaxpr/all_gather | solution.py:116
  15.7 43.4 %copy-start.45 = (f32[128]{0:T(128)}, f32[128]{0:T(128)S(1)}, u32[]{:S(2)}) copy-start(f32[128]{0:T(128)S(1)} %broadcast_multiply_fusion.8) | copy-start | bytes 1540 | tf_op jit(solution)/shard_map/while
  16.0 43.2 %copy-start.52 = (f32[128]{0:T(128)}, f32[128]{0:T(128)S(1)}, u32[]{:S(2)}) copy-start(f32[128]{0:T(128)S(1)} %fusion.373) | copy-start | bytes 1540 | tf_op jit(solution)/shard_map/while
  17.2 91.4 %all-gather.13.cloned.1.call-start = ((), (), s32[]{:S(2)}) async-start(), calls=%async_computation.16 | async-start | bytes 1310720 | tf_op jit(solution)/shard_map/while/body/eval_jaxpr/all_gather | solution.py:114
  18.9 106.5 %all-gather.15.cloned.1.call-start = ((), (), s32[]{:S(2)}) async-start(), calls=%async_computation.17 | async-start | bytes 1310720 | tf_op jit(solution)/shard_map/while/body/eval_jaxpr/all_gather | solution.py:119
  21.9 129.9 %all-gather.17.cloned.1.call-start = ((), (), s32[]{:S(2)}) async-start(), calls=%async_computation.18 | async-start | bytes 1310720 | tf_op jit(solution)/shard_map/while/body/eval_jaxpr/all_gather | solution.py:117
  24.8 161.8 %all-gather.19.cloned.1.call-start = ((), (), s32[]{:S(2)}) async-start(), calls=%async_computation.19 | async-start | bytes 1310720 | tf_op jit(solution)/shard_map/while/body/eval_jaxpr/all_gather | solution.py:142
  61.5 55.3 %copy-start.25 = (bf16[128,1024]{0,1:T(8,128)(2,1)}, bf16[128,1024]{0,1:T(8,128)(2,1)S(1)}, u32[]{:S(2)}) copy-start(bf16[128,1024]{0,1:T(8,128)(2,1)S(1)} %copy.114) | copy-start | bytes 786436 | tf_op jit(solution)/shard_map/while
  159.1 57.0 %all-gather.21.cloned.1.call-start = ((), (), s32[]{:S(2)}) async-start(), calls=%async_computation.20 | async-start | bytes 1310720 | tf_op jit(solution)/shard_map/while/body/eval_jaxpr/all_gather | solution.py:156
  161.4 90.6 %reduce-scatter.42.cloned.1.call-start = ((), (), s32[]{:S(2)}) async-start(), calls=%async_computation.21 | async-start | bytes 1310720 | tf_op jit(solution)/shard_map/while/body/eval_jaxpr/reduce_scatter | solution.py:162
  225.2 137.8 %reduce-scatter.56.cloned.1.call-start = ((), (), s32[]{:S(2)}) async-start(), calls=%async_computation.28 | async-start | bytes 1310720 | tf_op jit(solution)/shard_map/while/body/eval_jaxpr/reduce_scatter | solution.py:146
  229.5 135.3 %reduce-scatter.52.cloned.1.call-start = ((), (), s32[]{:S(2)}) async-start(), calls=%async_computation.26 | async-start | bytes 983040 | tf_op jit(solution)/shard_map/while
  274.0 95.4 %reduce-scatter.54.cloned.1.call-start = ((), (), s32[]{:S(2)}) async-start(), calls=%async_computation.27 | async-start | bytes 983040 | tf_op jit(solution)/shard_map/while
  283.0 91.2 %reduce-scatter.44.cloned.1.call-start = ((), (), s32[]{:S(2)}) async-start(), calls=%async_computation.22 | async-start | bytes 1310720 | tf_op jit(solution)/shard_map/while
  288.4 97.7 %reduce-scatter.46.cloned.1.call-start = ((), (), s32[]{:S(2)}) async-start(), calls=%async_computation.23 | async-start | bytes 1310720 | tf_op jit(solution)/shard_map/while
  293.9 120.4 %reduce-scatter.48.cloned.1.call-start = ((), (), s32[]{:S(2)}) async-start(), calls=%async_computation.24 | async-start | bytes 1310720 | tf_op jit(solution)/shard_map/while
  312.8 129.6 %reduce-scatter.50.cloned.1.call-start = ((), (), s32[]{:S(2)}) async-start(), calls=%async_computation.25 | async-start | bytes 1310720 | tf_op jit(solution)/shard_map/while
  390.8 51.5 %copy-start.57 = (f32[128]{0:T(128)S(1)}, f32[128]{0:T(128)}, u32[]{:S(2)}) copy-start(f32[128]{0:T(128)} %copy-done.56) | copy-start | bytes 1540 | tf_op jit(solution)/shard_map/while
  390.8 51.5 %copy-start.80 = (f32[128]{0:T(128)S(1)}, f32[128]{0:T(128)}, u32[]{:S(2)}) copy-start(f32[128]{0:T(128)} %copy-done.79) | copy-start | bytes 1540 | tf_op jit(solution)/shard_map/while
  392.3 52.8 %copy-start.73 = (f32[1024]{0:T(1024)S(1)}, f32[1024]{0:T(1024)}, u32[]{:S(2)}) copy-start(f32[1024]{0:T(1024)} %get-tuple-element.1197) | copy-start | bytes 12292 | tf_op jit(solution)/shard_map/while
  392.3 52.8 %copy-start.76 = (f32[1024]{0:T(1024)S(1)}, f32[1024]{0:T(1024)}, u32[]{:S(2)}) copy-start(f32[1024]{0:T(1024)} %get-tuple-element.1198) | copy-start | bytes 12292 | tf_op jit(solution)/shard_map/while
  392.3 52.8 %copy-start.21 = (bf16[2,1,128,1024]{3,2,1,0:T(8,128)(2,1)S(1)}, bf16[2,1,128,1024]{3,2,1,0:T(8,128)(2,1)}, u32[]{:S(2)}) copy-start(bf16[2,1,128,1024]{3,2,1,0:T(8,128)(2,1)} %get-tuple-element.1393) | copy-start | bytes 1572868 | tf_op jit(solution)/shard_map/while
  457.7 45.7 %copy-start.41 = (f32[8,2,22]{1,2,0:T(8,128)}, f32[8,2,22]{1,2,0:T(8,128)S(1)}, u32[]{:S(2)}) copy-start(f32[8,2,22]{1,2,0:T(8,128)S(1)} %get-tuple-element.1274) | copy-start | bytes 4228 | tf_op jit(solution)/shard_map/while
  457.7 90.5 %all-gather.11.cloned.1.call-start = ((), (), s32[]{:S(2)}) async-start(), calls=%async_computation.15 | async-start | bytes 1310720 | tf_op jit(solution)/shard_map/while/body/eval_jaxpr/all_gather | solution.py:116
  459.4 88.8 %all-gather.13.cloned.1.call-start = ((), (), s32[]{:S(2)}) async-start(), calls=%async_computation.16 | async-start | bytes 1310720 | tf_op jit(solution)/shard_map/while/body/eval_jaxpr/all_gather | solution.py:114
  461.2 103.9 %all-gather.15.cloned.1.call-start = ((), (), s32[]{:S(2)}) async-start(), calls=%async_computation.17 | async-start | bytes 1310720 | tf_op jit(solution)/shard_map/while/body/eval_jaxpr/all_gather | solution.py:119
  464.1 125.6 %all-gather.17.cloned.1.call-start = ((), (), s32[]{:S(2)}) async-start(), calls=%async_computation.18 | async-start | bytes 1310720 | tf_op jit(solution)/shard_map/while/body/eval_jaxpr/all_gather | solution.py:117
  467.0 157.5 %all-gather.19.cloned.1.call-start = ((), (), s32[]{:S(2)}) async-start(), calls=%async_computation.19 | async-start | bytes 1310720 | tf_op jit(solution)/shard_map/while/body/eval_jaxpr/all_gather | solution.py:142
  502.2 54.3 %copy-start.25 = (bf16[128,1024]{0,1:T(8,128)(2,1)}, bf16[128,1024]{0,1:T(8,128)(2,1)S(1)}, u32[]{:S(2)}) copy-start(bf16[128,1024]{0,1:T(8,128)(2,1)S(1)} %copy.114) | copy-start | bytes 786436 | tf_op jit(solution)/shard_map/while
  597.0 57.0 %all-gather.21.cloned.1.call-start = ((), (), s32[]{:S(2)}) async-start(), calls=%async_computation.20 | async-start | bytes 1310720 | tf_op jit(solution)/shard_map/while/body/eval_jaxpr/all_gather | solution.py:156
  599.3 90.6 %reduce-scatter.42.cloned.1.call-start = ((), (), s32[]{:S(2)}) async-start(), calls=%async_computation.21 | async-start | bytes 1310720 | tf_op jit(solution)/shard_map/while/body/eval_jaxpr/reduce_scatter | solution.py:162
  663.2 149.7 %reduce-scatter.56.cloned.1.call-start = ((), (), s32[]{:S(2)}) async-start(), calls=%async_computation.28 | async-start | bytes 1310720 | tf_op jit(solution)/shard_map/while/body/eval_jaxpr/reduce_scatter | solution.py:146
  667.4 147.2 %reduce-scatter.52.cloned.1.call-start = ((), (), s32[]{:S(2)}) async-start(), calls=%async_computation.26 | async-start | bytes 983040 | tf_op jit(solution)/shard_map/while
  711.9 107.3 %reduce-scatter.54.cloned.1.call-start = ((), (), s32[]{:S(2)}) async-start(), calls=%async_computation.27 | async-start | bytes 983040 | tf_op jit(solution)/shard_map/while
  720.9 103.1 %reduce-scatter.44.cloned.1.call-start = ((), (), s32[]{:S(2)}) async-start(), calls=%async_computation.22 | async-start | bytes 1310720 | tf_op jit(solution)/shard_map/while
  726.4 99.5 %reduce-scatter.46.cloned.1.call-start = ((), (), s32[]{:S(2)}) async-start(), calls=%async_computation.23 | async-start | bytes 1310720 | tf_op jit(solution)/shard_map/while
  731.8 120.2 %reduce-scatter.48.cloned.1.call-start = ((), (), s32[]{:S(2)}) async-start(), calls=%async_computation.24 | async-start | bytes 1310720 | tf_op jit(solution)/shard_map/while
  755.3 124.9 %reduce-scatter.50.cloned.1.call-start = ((), (), s32[]{:S(2)}) async-start(), calls=%async_computation.25 | async-start | bytes 1310720 | tf_op jit(solution)/shard_map/while
  830.5 49.7 %copy-start.57 = (f32[128]{0:T(128)S(1)}, f32[128]{0:T(128)}, u32[]{:S(2)}) copy-start(f32[128]{0:T(128)} %copy-done.56) | copy-start | bytes 1540 | tf_op jit(solution)/shard_map/while
  830.5 49.7 %copy-start.80 = (f32[128]{0:T(128)S(1)}, f32[128]{0:T(128)}, u32[]{:S(2)}) copy-start(f32[128]{0:T(128)} %copy-done.79) | copy-start | bytes 1540 | tf_op jit(solution)/shard_map/while
  832.0 50.9 %copy-start.73 = (f32[1024]{0:T(1024)S(1)}, f32[1024]{0:T(1024)}, u32[]{:S(2)}) copy-start(f32[1024]{0:T(1024)} %get-tuple-element.1197) | copy-start | bytes 12292 | tf_op jit(solution)/shard_map/while
  832.0 51.0 %copy-start.76 = (f32[1024]{0:T(1024)S(1)}, f32[1024]{0:T(1024)}, u32[]{:S(2)}) copy-start(f32[1024]{0:T(1024)} %get-tuple-element.1198) | copy-start | bytes 12292 | tf_op jit(solution)/shard_map/while
  832.0 51.0 %copy-start.21 = (bf16[2,1,128,1024]{3,2,1,0:T(8,128)(2,1)S(1)}, bf16[2,1,128,1024]{3,2,1,0:T(8,128)(2,1)}, u32[]{:S(2)}) copy-start(bf16[2,1,128,1024]{3,2,1,0:T(8,128)(2,1)} %get-tuple-element.1393) | copy-start | bytes 1572868 | tf_op jit(solution)/shard_map/while
  898.4 456.3 %all-reduce.3.cloned.1.call-start = ((), (), s32[]{:S(2)}) async-start(), calls=%async_computation.14 | async-start | bytes 25165824 | tf_op jit(solution)/shard_map/psum | solution.py:311
  899.0 455.7 %reduce-scatter.38.cloned.1.call-start = ((), (), s32[]{:S(2)}) async-start(), calls=%async_computation.12 | async-start | bytes 4718592 | tf_op jit(solution)/shard_map/reduce_scatter | solution.py:305
  899.7 455.0 %reduce-scatter.40.cloned.1.call-start = ((), (), s32[]{:S(2)}) async-start(), calls=%async_computation.13 | async-start | bytes 4718592 | tf_op jit(solution)/shard_map/reduce_scatter | solution.py:306
  900.3 558.4 %reduce-scatter.36.cloned.1.call-start = ((), (), s32[]{:S(2)}) async-start(), calls=%async_computation.11 | async-start | bytes 17301504 | tf_op jit(solution)/shard_map/reduce_scatter | solution.py:303
  (169 other events, 934.1 us)
Sparse Core Ops, SparseCore 0:
  18.5 43.2 all-gather.10
  63.4 27.5 all-gather.12
  92.5 30.3 all-gather.14
  124.4 27.3 all-gather.16
  159.2 27.4 all-gather.18
  188.6 27.4 all-gather.20
  225.3 26.6 reduce-scatter.41
  254.4 25.8 reduce-scatter.55
  282.6 21.9 reduce-scatter.51
  306.7 22.5 reduce-scatter.53
  331.6 26.4 reduce-scatter.43
  360.3 25.7 reduce-scatter.45
  388.4 25.7 reduce-scatter.47
  416.5 25.7 reduce-scatter.49
  460.4 39.7 all-gather.10
  501.6 26.9 all-gather.12
  530.0 30.1 all-gather.14
  561.7 27.9 all-gather.16
  597.1 27.4 all-gather.18
  626.6 27.4 all-gather.20
  663.3 26.5 reduce-scatter.41
  692.3 25.8 reduce-scatter.55
  720.5 21.9 reduce-scatter.51
  744.6 22.5 reduce-scatter.53
  769.5 26.4 reduce-scatter.43
  798.2 25.7 reduce-scatter.45
  826.2 25.7 reduce-scatter.47
  854.4 25.7 reduce-scatter.49
  903.8 51.9 reduce-scatter.37
  959.9 51.8 reduce-scatter.39
  1014.7 443.9 reduce-scatter.35
Sparse Core Ops, SparseCore 1:
  905.5 449.1 all-reduce.2
where the time goes:
time: 1480 us
  waiting for transfers between devices  797 us (54%)
  matrix products  233 us (16%)
  local copies, waits for them, and re-layouts  197 us (13%)
  blocking collectives  145 us (10%)
  other arithmetic  78.2 us (5%)
  between operations  16.1 us (1%)
    psum x1, waiting for transfers between devices, on_device(): lax.psum((totals[13], totals[14], totals[0], totals[1], totals[7], totals...  400 us
    reduce_scatter x1, waiting for transfers between devices, on_device(): lax.psum_scatter(attn_grad, ('dp', 'ffn'), scatter_dimension=0, tiled=True)  104 us
    while x40, waiting for transfers between devices  104 us
    dot_general x22, matrix products, contract_rows(): lax.dot_general(left, right, (((0,), (0,)), ((), ())), preferred_element_...  78.6 us
    all_gather x2, blocking collectives, micro_batch(): lax.all_gather(own_keys[1], 'ffn', axis=0, tiled=True)  61.9 us
    while x348, local copies, waits for them, and re-layouts  60.1 us
    dot_general x22, matrix products, matmul(): return jnp.dot(left, right, preferred_element_type=jnp.float32)  57.1 us
    all_gather x2, waiting for transfers between devices, micro_batch(): lax.all_gather(own_values[0], 'ffn', axis=0, tiled=True)  50.9 us
  transfers between devices with their start and end apart: 32, of which 15 were waited for; matrix products, arithmetic and copies ran while one was open for 28% of the time, Pallas kernels for 0%

commit v1 on v0

v1 whole, which is shorter than its diff:
```python
import functools
import math

import jax
import jax.numpy as jnp
from jax import lax
from jax.experimental import pallas as pl
from jax.experimental.pallas import tpu as pltpu
from jax.sharding import PartitionSpec as P

D = 1024
H = 8
HD = 128
SEG = 512
M = 384
CM = 512
PW = 64
KR = 1408
NB = 22
OH = 4
HALF = OH * HD
EPSILON = 1e-05
MASKED = -1e30
SCALE = HD ** (-0.5)
BF = jnp.bfloat16
F32 = jnp.float32


def statistics(rows_in):
    centre = jnp.mean(rows_in, axis=-1, keepdims=True)
    centred = rows_in - centre
    variance = jnp.mean(centred * centred, axis=-1, keepdims=True)
    inverse = lax.rsqrt(variance + EPSILON)
    return centred * inverse, inverse


def matmul(left, right):
    return jnp.dot(left, right, preferred_element_type=F32)


def contract_rows(left, right):
    return lax.dot_general(left, right, (((0,), (0,)), ((), ())), preferred_element_type=F32)


def times_transposed(left, right):
    return lax.dot_general(left, right, (((1,), (1,)), ((), ())), preferred_element_type=F32)


def norm_pull(xhat, inverse, scaled):
    mean_a = jnp.mean(scaled, axis=-1, keepdims=True)
    mean_b = jnp.mean(scaled * xhat, axis=-1, keepdims=True)
    return (scaled - mean_a - xhat * mean_b) * inverse


def attention_forward_kernel(counts, q_ref, k_ref, v_ref, bias_ref, o_ref, p_ref):
    comp_low = CM - counts[0]
    mem_low = CM + M - counts[1]
    for tile in range(SEG // HD):
        cols = slice(tile * HD, (tile + 1) * HD)
        seen = CM + M + (tile + 1) * HD
        raw = times_transposed(k_ref[:seen, :], q_ref[cols, :]) * SCALE
        blocks = seen // PW
        raw = (
            raw.reshape(blocks, PW, HD) + bias_ref[0, :blocks, cols].reshape(blocks, 1, HD)
        ).reshape(seen, HD)
        key_pos = lax.broadcasted_iota(jnp.int32, (seen, HD), 0)
        query_pos = CM + M + tile * HD + lax.broadcasted_iota(jnp.int32, (seen, HD), 1)
        low = jnp.where(key_pos < CM, comp_low, jnp.where(key_pos < CM + M, mem_low, 0))
        scores = jnp.where((key_pos >= low) & (key_pos <= query_pos), raw, MASKED)
        top = jnp.max(scores, axis=0, keepdims=True)
        expanded = jnp.exp(scores - top)
        total = jnp.sum(expanded, axis=0, keepdims=True)
        attention = (expanded * (1.0 / total)).astype(BF)
        p_ref[0, :seen, cols] = attention
        if seen < KR:
            p_ref[0, seen:, cols] = jnp.zeros((KR - seen, HD), BF)
        mixed = contract_rows(v_ref[:seen, :], attention)
        o_ref[cols, :] = mixed.T.astype(BF)


def attention_forward(counts, queries, keys, values, bias):
    return pl.pallas_call(
        attention_forward_kernel,
        grid=(OH,),
        in_specs=[
            pl.BlockSpec(memory_space=pltpu.SMEM),
            pl.BlockSpec((SEG, HD), lambda h: (0, h)),
            pl.BlockSpec((KR, HD), lambda h: (0, h)),
            pl.BlockSpec((KR, HD), lambda h: (0, h)),
            pl.BlockSpec((1, NB, SEG), lambda h: (h, 0, 0)),
        ],
        out_specs=[
            pl.BlockSpec((SEG, HD), lambda h: (0, h)),
            pl.BlockSpec((1, KR, SEG), lambda h: (h, 0, 0)),
        ],
        out_shape=[
            jax.ShapeDtypeStruct((SEG, HALF), BF),
            jax.ShapeDtypeStruct((OH, KR, SEG), BF),
        ],
        cost_estimate=pl.CostEstimate(
            flops=4 * OH * SEG * KR * HD, bytes_accessed=10 << 20, transcendentals=OH * SEG * KR
        ),
        name="attention_forward",
    )(counts, queries, keys, values, bias)


def attention_backward_kernel(
    p_ref, q_ref, k_ref, v_ref, g_ref, dq_ref, dk_ref, dv_ref, sums_ref, ds_ref
):
    for tile in range(SEG // HD):
        cols = slice(tile * HD, (tile + 1) * HD)
        seen = CM + M + (tile + 1) * HD
        blocks = seen // PW
        attention = p_ref[0, :seen, cols].astype(F32)
        grad_attention = times_transposed(v_ref[:seen, :], g_ref[cols, :])
        inner = jnp.sum(attention * grad_attention, axis=0, keepdims=True)
        grad_scores = (attention * (grad_attention - inner)).astype(BF)
        ds_ref[:seen, cols] = grad_scores
        sums_ref[0, :blocks, cols] = jnp.sum(
            grad_scores.astype(F32).reshape(blocks, PW, HD), axis=1
        )
        if seen < KR:
            ds_ref[seen:, cols] = jnp.zeros((KR - seen, HD), BF)
            sums_ref[0, blocks:, cols] = jnp.zeros((NB - blocks, HD), F32)
        grad_query = contract_rows(k_ref[:seen, :], grad_scores) * SCALE
        dq_ref[cols, :] = grad_query.T.astype(BF)
    dk_ref[...] = (matmul(ds_ref[...], q_ref[...]) * SCALE).astype(BF)
    dv_ref[...] = matmul(p_ref[0], g_ref[...]).astype(BF)


def attention_backward(attention, queries, keys, values, grad_mixed):
    rows_of = lambda n: pl.BlockSpec((n, HD), lambda h: (0, h))
    return pl.pallas_call(
        attention_backward_kernel,
        grid=(OH,),
        in_specs=[
            pl.BlockSpec((1, KR, SEG), lambda h: (h, 0, 0)),
            rows_of(SEG),
            rows_of(KR),
            rows_of(KR),
            rows_of(SEG),
        ],
        out_specs=[
            rows_of(SEG),
            rows_of(KR),
            rows_of(KR),
            pl.BlockSpec((1, NB, SEG), lambda h: (h, 0, 0)),
        ],
        out_shape=[
            jax.ShapeDtypeStruct((SEG, HALF), BF),
            jax.ShapeDtypeStruct((KR, HALF), BF),
            jax.ShapeDtypeStruct((KR, HALF), BF),
            jax.ShapeDtypeStruct((OH, NB, SEG), F32),
        ],
        scratch_shapes=[pltpu.VMEM((KR, SEG), BF)],
        cost_estimate=pl.CostEstimate(
            flops=8 * OH * SEG * KR * HD, bytes_accessed=14 << 20, transcendentals=0
        ),
        name="attention_backward",
    )(attention, queries, keys, values, grad_mixed)


def feed_forward_kernel(
    place, x_ref, gy_ref, up_ref, bias_ref, down_ref, res_ref,
    part_ref, grad_ref, sum_ref, weights_ref, up_acc, down_acc,
):
    block = pl.program_id(0)
    rows = x_ref[0]
    gy = gy_ref[0]
    hidden = matmul(rows, up_ref[...]) + bias_ref[...]
    normal = 0.5 * (1.0 + lax.erf(hidden * math.sqrt(0.5)))
    slope = normal + hidden * jnp.exp(-0.5 * hidden * hidden) * (1.0 / math.sqrt(2.0 * math.pi))
    activated = (hidden * normal).astype(BF)
    part = matmul(activated, down_ref[...])
    own = (block == place[0]).astype(F32)
    part_ref[0] = (part + own * res_ref[...]).astype(BF)
    grad_hidden = times_transposed(gy, down_ref[...])
    grad_pre = (grad_hidden * slope).astype(BF)
    grad_ref[0] = times_transposed(grad_pre, up_ref[...]).astype(BF)
    column_sum = jnp.sum(grad_pre.astype(F32), axis=0, keepdims=True)
    up_part = contract_rows(rows, grad_pre)
    down_part = contract_rows(gy, activated)

    @pl.when(block == 0)
    def _():
        sum_ref[...] = column_sum
        up_acc[...] = up_part
        down_acc[...] = down_part

    @pl.when(block > 0)
    def _():
        sum_ref[...] += column_sum
        up_acc[...] += up_part
        down_acc[...] += down_part

    @pl.when(block == pl.num_programs(0) - 1)
    def _():
        pieces, _, height, _ = weights_ref.shape
        for piece in range(pieces):
            span = slice(piece * height, (piece + 1) * height)
            weights_ref[piece, 0] = up_acc[span, :].astype(BF)
            weights_ref[piece, 1] = down_acc[span, :].astype(BF)


def feed_forward(place, rows, gy, w_up, b_up, w_down, residual, pieces):
    blocks, height, _ = rows.shape
    hidden = w_up.shape[1]
    whole = lambda a, b: pl.BlockSpec((a, b), lambda i: (0, 0))
    each = pl.BlockSpec((1, height, D), lambda i: (i, 0, 0))
    return pl.pallas_call(
        feed_forward_kernel,
        grid=(blocks,),
        in_specs=[
            pl.BlockSpec(memory_space=pltpu.SMEM),
            each,
            each,
            whole(D, hidden),
            whole(1, hidden),
            whole(hidden, D),
            whole(height, D),
        ],
        out_specs=[
            each,
            each,
            whole(1, hidden),
            pl.BlockSpec((pieces, 2, D // pieces, hidden), lambda i: (0, 0, 0, 0)),
        ],
        out_shape=[
            jax.ShapeDtypeStruct((blocks, height, D), BF),
            jax.ShapeDtypeStruct((blocks, height, D), BF),
            jax.ShapeDtypeStruct((1, hidden), F32),
            jax.ShapeDtypeStruct((pieces, 2, D // pieces, hidden), BF),
        ],
        scratch_shapes=[pltpu.VMEM((D, hidden), F32), pltpu.VMEM((D, hidden), F32)],
        compiler_params=pltpu.CompilerParams(vmem_limit_bytes=60 << 20),
        cost_estimate=pl.CostEstimate(
            flops=12 * blocks * height * D * hidden,
            bytes_accessed=20 << 20,
            transcendentals=2 * blocks * height * hidden,
        ),
        name="feed_forward",
    )(place, rows, gy, w_up, b_up.reshape(1, hidden), w_down, residual)


def on_device(
    seg_input,
    memory,
    compressed,
    mem_fill,
    comp_fill,
    attn_gain,
    attn_shift,
    attn_weights,
    rel_table,
    ffn_gain,
    ffn_shift,
    w_up,
    b_up,
    w_down,
    b_down,
    conv_weight,
    conv_bias,
    out_grad,
    comp_grad,
):
    streams = lax.axis_size("dp")
    layers = lax.axis_size("ffn")
    stream = lax.axis_index("dp")
    layer = lax.axis_index("ffn")
    core = stream % 2
    micros = seg_input.shape[0]
    seg_rows, mem_rows, comp_rows = seg_input.shape[2], memory.shape[2], compressed.shape[2]
    hidden_local = w_up.shape[1]
    groups = streams // 2
    twins = [(i, i ^ 1) for i in range(streams)]
    first = core == 0

    def swap(value):
        return lax.ppermute(value, "dp", twins)

    def by_core(mine, other, axis):
        return jnp.where(
            first, jnp.stack([mine, other], axis=axis), jnp.stack([other, mine], axis=axis)
        )

    def halves(value):
        split = value.reshape(micros, 2, value.shape[1] // 2, D)
        return (
            lax.dynamic_index_in_dim(split, core, 1, keepdims=False),
            lax.dynamic_index_in_dim(split, 1 - core, 1, keepdims=False),
        )

    seg, mem, comp = seg_input[:, 0], memory[:, 0], compressed[:, 0]
    gy_own, comp_cot = out_grad[:, 0], comp_grad[:, 0]

    kept, sent = zip(*[halves(x) for x in (comp, mem, seg, gy_own)])
    came = swap(jnp.concatenate(sent, axis=1))
    kept = jnp.concatenate(kept, axis=1)
    pairs = by_core(kept, came, 1).reshape(2 * micros, -1, D)
    hc, hm, hs = comp_rows // 2, mem_rows // 2, seg_rows // 2
    source_rows = hc + hm + hs
    source = lax.all_to_all(
        pairs[:, :source_rows], "ffn", split_axis=0, concat_axis=0, tiled=True
    )
    gy_all = lax.all_gather(pairs[:, source_rows:], "ffn", axis=1, tiled=True)

    fills = jnp.concatenate([comp_fill, mem_fill], axis=1).astype(F32)
    twin_fills = swap(fills)
    pair_micro, pair_core = layer // 2, layer % 2
    counts = lax.dynamic_index_in_dim(
        jnp.where(pair_core == core, fills, twin_fills), pair_micro, 0, keepdims=False
    ).astype(jnp.int32)

    memory_pos = layer * mem_rows + jnp.arange(mem_rows, dtype=jnp.int32)
    alive = memory_pos[None, :] >= M - mem_fill
    flat = jnp.where(alive[:, :, None], mem, jnp.zeros_like(mem))
    flat = flat.reshape(micros * (mem_rows // 3), 3 * D)
    new_compressed = (matmul(flat, conv_weight) + conv_bias).astype(BF)
    new_compressed = new_compressed.reshape(micros, 1, mem_rows // 3, D)
    cot_rows = comp_cot.reshape(-1, D)
    conv_part = contract_rows(flat, cot_rows).astype(BF)
    conv_part = lax.psum_scatter(conv_part, "dp", scatter_dimension=0, tiled=True)
    conv_part = lax.psum_scatter(conv_part, "ffn", scatter_dimension=0, tiled=True)
    conv_grad = lax.all_gather(conv_part, ("dp", "ffn"), axis=0, tiled=True).astype(F32)
    conv_bias_part = jnp.sum(cot_rows.astype(F32), axis=0)
    down_bias_part = jnp.sum(gy_own.astype(F32), axis=(0, 1))

    source_f = source.reshape(layers * source_rows, D).astype(F32)
    source_hat, source_inverse = statistics(source_f)
    normed_half = (source_hat * attn_gain + attn_shift).astype(BF)
    normed_pair = by_core(normed_half, swap(normed_half), 0)
    normed_pair = normed_pair.reshape(2, layers, source_rows, D)
    sections = []
    start = 0
    for height in (hc, hm, hs):
        piece = normed_pair[:, :, start : start + height]
        sections.append(piece.transpose(1, 0, 2, 3).reshape(2 * layers * height, D))
        start += height
    normed = jnp.concatenate(sections, axis=0)
    own_columns = lax.dynamic_slice(attn_weights, (0, core * HALF), (4 * D, HALF))
    w_query, w_key, w_value = own_columns[:D], own_columns[D : 2 * D], own_columns[2 * D : 3 * D]
    w_out = attn_weights[3 * D :]
    w_out_rows = lax.dynamic_slice(attn_weights, (3 * D + core * HALF, 0), (HALF, D))
    normed_queries = normed[CM + M :]
    queries = matmul(normed_queries, w_query).astype(BF)
    keys = matmul(normed, w_key).astype(BF)
    values = matmul(normed, w_value).astype(BF)

    table = lax.dynamic_slice(rel_table, (core * OH, 0), (OH, NB))
    query_blocks = SEG // PW
    first_block = (CM + M) // PW
    extended = jnp.concatenate([jnp.full((OH, query_blocks - 1), MASKED, F32), table], axis=1)
    offset = first_block + query_blocks - 1
    bias = jnp.stack(
        [extended[:, offset - b : offset - b + query_blocks] for b in range(NB)], axis=1
    )
    bias = jnp.broadcast_to(bias[..., None], (OH, NB, query_blocks, PW)).reshape(OH, NB, SEG)
    mixed_own, attention = attention_forward(counts, queries, keys, values, bias)
    mixed = by_core(mixed_own, swap(mixed_own), 1).reshape(SEG, D)

    def own_rows(value):
        split = value.reshape(layers, 2, hs, D)
        return lax.dynamic_index_in_dim(split, core, 1, keepdims=False).reshape(layers * hs, D)

    segment_half = source.reshape(layers, source_rows, D)[:, hc + hm :]
    segment_half = segment_half.reshape(layers * hs, D).astype(F32)
    residual = segment_half + matmul(own_rows(mixed), w_out)
    residual_hat, residual_inverse = statistics(residual)
    ffn_in = (residual_hat * ffn_gain + ffn_shift).astype(BF)

    ffn_rows = lax.all_gather(ffn_in, "ffn", axis=0, tiled=True).reshape(layers, layers * hs, D)
    place = layer.reshape(1).astype(jnp.int32)
    parts, grad_parts, up_bias_part, weight_parts = feed_forward(
        place, ffn_rows, gy_all, w_up, b_up, w_down, residual + b_down, streams
    )
    weight_sum = lax.psum_scatter(weight_parts, "dp", scatter_dimension=0, tiled=True)[0]
    weight_sum = weight_sum.astype(F32)
    up_grad = weight_sum[0]
    down_grad = weight_sum[1].T
    layer_rows = lax.psum_scatter(parts, "ffn", scatter_dimension=1, tiled=True)
    grad_ffn_in = lax.psum_scatter(
        grad_parts.reshape(layers * layers * hs, D), "ffn", scatter_dimension=0, tiled=True
    ).astype(F32)

    def to_owners(value):
        split = value.reshape(micros, 2, hs, D)
        stay = lax.dynamic_index_in_dim(split, core, 1, keepdims=False)
        other = swap(lax.dynamic_index_in_dim(split, 1 - core, 1, keepdims=False))
        return by_core(stay, other, 1).reshape(micros, 1, 2 * hs, D)

    layer_out = to_owners(layer_rows)

    ffn_gain_part = jnp.sum(grad_ffn_in * residual_hat, axis=0)
    ffn_shift_part = jnp.sum(grad_ffn_in, axis=0)
    gy_half = lax.dynamic_index_in_dim(gy_all, layer, 0, keepdims=False).astype(F32)
    grad_residual = gy_half + norm_pull(residual_hat, residual_inverse, grad_ffn_in * ffn_gain)
    branch_half = grad_residual.astype(BF).reshape(layers, hs, D)
    grad_branch = by_core(branch_half, swap(branch_half), 1).reshape(SEG, D)

    grad_mixed = times_transposed(grad_branch, w_out_rows).astype(BF)
    branch_columns = lax.dynamic_slice(grad_branch, (0, core * HALF), (SEG, HALF))
    out_grad_part = contract_rows(mixed, branch_columns)
    grad_query, grad_key, grad_value, sums = attention_backward(
        attention, queries, keys, values, grad_mixed
    )
    query_part = contract_rows(normed_queries, grad_query)
    key_part = contract_rows(normed, grad_key)
    value_part = contract_rows(normed, grad_value)
    grad_normed = (
        times_transposed(grad_query, w_query)
        + times_transposed(grad_key[CM + M :], w_key)
        + times_transposed(grad_value[CM + M :], w_value)
    ).astype(BF)
    grad_normed = grad_normed.reshape(layers, 2, hs, D)
    grad_stay = lax.dynamic_index_in_dim(grad_normed, core, 1, keepdims=False).astype(F32)
    grad_came = swap(lax.dynamic_index_in_dim(grad_normed, 1 - core, 1, keepdims=False))
    grad_normed = (grad_stay + grad_came.astype(F32)).reshape(layers * hs, D)
    segment_hat = source_hat.reshape(layers, source_rows, D)[:, hc + hm :].reshape(-1, D)
    segment_inverse = source_inverse.reshape(layers, source_rows, 1)[:, hc + hm :].reshape(-1, 1)
    grad_segment = grad_residual + norm_pull(
        segment_hat, segment_inverse, grad_normed * attn_gain
    )
    grad_segment = lax.all_to_all(
        grad_segment.astype(BF).reshape(layers, hs, D),
        "ffn", split_axis=0, concat_axis=0, tiled=True,
    )
    seg_grad = to_owners(grad_segment).astype(F32)

    def column_sums(value):
        return jnp.sum(value.astype(F32), axis=0)

    shift_part = (
        jnp.sum(w_query.astype(F32) * column_sums(grad_query), axis=1)
        + jnp.sum(w_key.astype(F32) * column_sums(grad_key), axis=1)
        + jnp.sum(w_value.astype(F32) * column_sums(grad_value), axis=1)
    )
    product = (
        jnp.sum(w_query.astype(F32) * query_part, axis=1)
        + jnp.sum(w_key.astype(F32) * key_part, axis=1)
        + jnp.sum(w_value.astype(F32) * value_part, axis=1)
    )
    gain_part = (product - attn_shift * shift_part) / attn_gain

    stack = jnp.stack([query_part, key_part, value_part, out_grad_part]).astype(BF)
    bits = streams.bit_length() - 1
    piece_rows = 4 * D // (streams * layers)
    chunks = stack.reshape((2,) * (bits - 1) + (2, layers, piece_rows, HALF))

    def reduce_groups(value, order):
        left = list(range(bits - 1, 0, -1))
        for bit in order:
            axis = left.index(bit)
            mine = (stream >> bit) & 1
            stay = lax.dynamic_index_in_dim(value, mine, axis, keepdims=False)
            goes = lax.dynamic_index_in_dim(value, 1 - mine, axis, keepdims=False)
            other = lax.ppermute(goes, "dp", [(i, i ^ (1 << bit)) for i in range(streams)])
            value = (stay.astype(F32) + other.astype(F32)).astype(BF)
            left.pop(axis)
        return value

    order = list(range(1, bits))
    lead = (slice(None),) * (bits - 1)
    low = reduce_groups(chunks[lead + (0,)], order)
    high = reduce_groups(chunks[lead + (1,)], order[::-1])
    both = jnp.stack([low, high], axis=1)
    both = lax.psum_scatter(both, "ffn", scatter_dimension=0, tiled=True)[0]
    stay = lax.dynamic_index_in_dim(both, core, 0, keepdims=False)
    other = swap(lax.dynamic_index_in_dim(both, 1 - core, 0, keepdims=False))
    attn_weights_grad = by_core(stay, other, 1).reshape(piece_rows, D).astype(F32)

    tile_sums = jnp.sum(sums.reshape(OH, NB, query_blocks, PW), axis=-1)
    distance = (
        first_block
        + jnp.arange(query_blocks, dtype=jnp.int32)[None, :]
        - jnp.arange(NB, dtype=jnp.int32)[:, None]
    )
    one_hot = (distance[:, :, None] == jnp.arange(NB, dtype=jnp.int32)).astype(F32)
    table_part = jnp.einsum("hkq,kqn->hn", tile_sums, one_hot, precision=lax.Precision.HIGHEST)
    table_row = lax.dynamic_update_slice(jnp.zeros((H, NB), F32), table_part, (core * OH, 0))
    table_row = jnp.pad(table_row.reshape(-1), (0, D - H * NB))
    up_bias_rows = lax.dynamic_update_slice(
        jnp.zeros((layers, hidden_local), F32), up_bias_part, (layer, 0)
    ).reshape(-1, D)
    up_bias_count = up_bias_rows.shape[0]
    small = jnp.concatenate(
        [
            jnp.stack(
                [gain_part, shift_part, ffn_gain_part, ffn_shift_part, down_bias_part,
                 conv_bias_part, table_row]
            ),
            up_bias_rows,
        ]
    )
    for bit in range(bits):
        small = small + lax.ppermute(small, "dp", [(i, i ^ (1 << bit)) for i in range(streams)])
    for bit in range(layers.bit_length() - 1):
        small = small + lax.ppermute(small, "ffn", [(i, i ^ (1 << bit)) for i in range(layers)])
    return (
        layer_out,
        new_compressed,
        seg_grad,
        small[0],
        small[1],
        attn_weights_grad,
        small[6, : H * NB].reshape(H, NB),
        small[2],
        small[3],
        up_grad,
        small[7 : 7 + up_bias_count].reshape(-1),
        down_grad,
        small[4],
        conv_grad,
        small[5],
    )


def solution(mesh):
    return jax.shard_map(
        on_device,
        mesh=mesh,
        in_specs=(
            P(None, "dp", "ffn", None),
            P(None, "dp", "ffn", None),
            P(None, "dp", "ffn", None),
            P(None, "dp"),
            P(None, "dp"),
            P(),
            P(),
            P(),
            P(),
            P(),
            P(),
            P(None, "ffn"),
            P("ffn"),
            P("ffn", None),
            P(),
            P(),
            P(),
            P(None, "dp", "ffn", None),
            P(None, "dp", "ffn", None),
        ),
        out_specs=(
            P(None, "dp", "ffn", None),
            P(None, "dp", "ffn", None),
            P(None, "dp", "ffn", None),
            P(),
            P(),
            P(("dp", "ffn"), None),
            P(),
            P(),
            P(),
            P("dp", "ffn"),
            P(),
            P("ffn", "dp"),
            P(),
            P(),
            P(),
        ),
        check_vma=False,
    )
```

time: 1480 us -> 473 us (0.32)
  waiting for transfers between devices: 797 us -> 255 us
  matrix products: 233 us -> 42.2 us
  local copies, waits for them, and re-layouts: 197 us -> 35.5 us
  blocking collectives: 145 us -> 0 us
  Pallas kernels: 0 us -> 46.8 us
  other arithmetic: 78.2 us -> 47 us
  starting transfers between devices: 2.46 us -> 24.8 us
    psum x1 -> x0, waiting for transfers between devices: 400 us -> none  [on_device(): lax.psum((totals[13], totals[14], totals[0], totals[1], totals[7], totals...]
    all_gather x4 -> x0, blocking collectives: 104 us -> none  [the longest x2 61.9 us: micro_batch(): lax.all_gather(own_keys[1], 'ffn', axis=0, tiled=True)]
    while x40 -> x0, waiting for transfers between devices: 104 us -> none
    reduce_scatter x7 -> x6, waiting for transfers between devices: 149 us -> 56.4 us  [the longest x1 40.4 us: on_device(): lax.psum_scatter(grad_parts.reshape(layers * layers * hs, D), 'ffn', scat...]
    dot_general x37 -> x6, matrix products: 108 us -> 19.1 us  [the longest x5 18.9 us: matmul(): return jnp.dot(left, right, preferred_element_type=F32)]
    dot_general x22 -> x5, matrix products: 78.6 us -> 14 us  [contract_rows(): lax.dot_general(left, right, (((0,), (0,)), ((), ())), preferred_element_...]
    while x348 -> x0, local copies, waits for them, and re-layouts: 60.1 us -> none
    ppermute x0 -> x18, waiting for transfers between devices: none -> 49.3 us  [the longest x4 32.9 us: reduce_groups(): lax.ppermute(goes, 'dp', [(i, i ^ 1 << bit) for i in range(streams)])]
  transfers between devices with their start and end apart: 32 -> 29, of which waited for: 15 -> 16; matrix products, arithmetic and copies ran while one was open for 28% -> 23% of each run, Pallas kernels for 0% -> 10%
where the time goes in v1:
time: 473 us; the launch traced here: 468 us
  waiting for transfers between devices  255 us (54%)
  other arithmetic  47 us (10%)
  Pallas kernels  46.8 us (10%)
  matrix products  42.2 us (9%)
  local copies, waits for them, and re-layouts  35.5 us (8%)
  starting transfers between devices  24.8 us (5%)
  between operations  16.8 us (4%)
    all_gather x1, waiting for transfers between devices, on_device(): lax.all_gather(conv_part, ('dp', 'ffn'), axis=0, tiled=True).astype(F32)  66.9 us
    all_gather x1, waiting for transfers between devices, on_device(): lax.all_gather(ffn_in, 'ffn', axis=0, tiled=True)  46.9 us
    reduce_scatter x1, waiting for transfers between devices, on_device(): lax.psum_scatter(grad_parts.reshape(layers * layers * hs, D), 'ffn', scat...  40.4 us
    all_to_all x1, waiting for transfers between devices, on_device(): lax.all_to_all(pairs[:, :source_rows], 'ffn', split_axis=0, concat_axis=0...  33.7 us
    ppermute x4, waiting for transfers between devices, reduce_groups(): lax.ppermute(goes, 'dp', [(i, i ^ 1 << bit) for i in range(streams)])  32.9 us
    pallas_call x1, Pallas kernels, feed_forward(): pl.pallas_call(feed_forward_kernel, grid=(blocks,), in_specs=[pl.BlockSpe...  23.1 us
    dot_general x5, matrix products, matmul(): return jnp.dot(left, right, preferred_element_type=F32)  18.9 us
    reduce_scatter x1, waiting for transfers between devices, on_device(): both = lax.psum_scatter(both, 'ffn', scatter_dimension=0, tiled=True)[0]  15.9 us
  transfers between devices with their start and end apart: 29, of which 16 were waited for; matrix products, arithmetic and copies ran while one was open for 23% of the time, Pallas kernels for 10%

profile of v1, /device:TPU:0, one launch (start us, length us, event | category | flops | bytes accessed | tf_op | source)
XLA Modules:
  0.0 468.1 jit_solution(15031190160362206207)
XLA Ops:
  12.7 1.8 collective-permute-done
  14.5 1.9 maximum_select_fusion.1
  17.6 6.4 %all-to-all-start = ((bf16[4,176,1024]{2,1,0:T(8,128)(2,1)}), bf16[4,176,1024]{2,1,0:T(8,128)(2,1)S(1)}, u32[]{:S(2)}, u32[]{:S(2)}) async-start(bf16[4,176,1024]{2,1,0:T(8,128)(2,1)} %slice.194), calls=%async_computation | async-start | bytes 2883584 | tf_op jit(solution)/shard_map/all_to_all | solution.py:302
  24.7 33.7 %all-to-all-done = bf16[4,176,1024]{2,1,0:T(8,128)(2,1)S(1)} async-done(((bf16[4,176,1024]{2,1,0:T(8,128)(2,1)}), bf16[4,176,1024]{2,1,0:T(8,128)(2,1)S(1)}, u32[]{:S(2)}, u32[]{:S(2)}) %all-to-all-start) | async-done | bytes 1441824 | tf_op jit(solution)/shard_map/all_to_all | solution.py:302
  60.0 1.7 fusion.3
  63.1 1.8 reshape.507
  65.0 1.7 copy.111.bias_ref
  68.8 2.3 subtract_multiply_fusion
  71.0 2.3 maximum_select_fusion
  74.0 3.6 convolution_convert_fusion.5.q_ref
  77.6 4.0 convolution_convert_fusion.1.v_ref
  81.6 4.1 convolution_convert_fusion.2.k_ref
  85.7 10.8 %attention_forward.1 = (bf16[512,512]{1,0:T(8,128)(2,1)}, bf16[4,1408,512]{2,1,0:T(8,128)(2,1)}) custom-call(s32[2]{0:T(128)} %fusion.59.counts, bf16[512,512]{1,0:T(8,128)(2,1)} %convolution_convert_fusion.5.q_ref, bf16[1408,512]{1,0:T(8,128)(2,1)} %convolution_convert_fusion.2.k_ref, bf16[1408,512]{1,0:T(8,128)(2,1)} %convolution_convert_fusion.1.v_ref, ...), custom_call_target="tpu_custom_call" | custom-call | flops 1476395008 | bytes 10485760 | tf_op jit(solution)/shard_map/attention_forward/pallas_call | solution.py:82
  97.0 1.7 collective-permute-done.3
  103.9 2.4 fusion.68
  108.6 4.5 convolution_convert_fusion
  113.5 46.9 %all-gather.4.cloned.1.call-done = bf16[1024,1024]{1,0:T(8,128)(2,1)} async-done(((bf16[256,1024]{1,0:T(8,128)(2,1)}), bf16[1024,1024]{1,0:T(8,128)(2,1)}) %all-gather.4.cloned.1.call-update) | async-done | bytes 2097168 | tf_op jit(solution)/shard_map/all_gather | solution.py:371
  160.4 23.1 %feed_forward.1 = (bf16[4,256,1024]{2,1,0:T(8,128)(2,1)}, bf16[4,256,1024]{2,1,0:T(8,128)(2,1)}, f32[1,1024]{1,0:T(1,128)}, bf16[8,2,128,1024]{3,2,1,0:T(8,128)(2,1)}) custom-call(s32[1]{0:T(128)} %bitcast.place, bf16[4,256,1024]{2,1,0:T(8,128)(2,1)} %bitcast.317, bf16[4,256,1024]{2,1,0:T(8,128)(2,1)} %all-gather.6.cloned.1.call-done.gy_ref, ...), custom_call_target="tpu_custom_call" | custom-call | flops 12884901888 | bytes 20971520 | tf_op jit(solution)/shard_map/feed_forward/pallas_call | solution.py:210
  184.9 40.4 %reduce-scatter.9.cloned.1.call-done = bf16[256,1024]{1,0:T(8,128)(2,1)} async-done(((bf16[1024,1024]{1,0:T(8,128)(2,1)}), bf16[256,1024]{1,0:T(8,128)(2,1)}) %reduce-scatter.9.cloned.1.call-update) | async-done | bytes 524304 | tf_op jit(solution)/shard_map/reduce_scatter | solution.py:381
  226.9 2.6 fusion.64
  233.6 2.8 convolution_convert_fusion.4.g_ref
  236.4 12.9 %attention_backward.1 = (bf16[512,512]{1,0:T(8,128)(2,1)}, bf16[1408,512]{1,0:T(8,128)(2,1)}, bf16[1408,512]{1,0:T(8,128)(2,1)}, f32[4,22,512]{2,1,0:T(8,128)}) custom-call(bf16[4,1408,512]{2,1,0:T(8,128)(2,1)} %get-tuple-element.28.p_ref, bf16[512,512]{1,0:T(8,128)(2,1)} %convolution_convert_fusion.5.q_ref, ...), custom_call_target="tpu_custom_call" | custom-call | flops 2952790016 | bytes 14680064 | tf_op jit(solution)/shard_map/attention_backward/pallas_call | solution.py:133
  250.6 1.8 convert_reduce_fusion
  253.4 3.0 fusion.62
  256.5 1.8 fusion.63
  258.3 3.9 fusion.6
  265.5 1.6 collective-permute-start.13
  269.7 21.5 %collective-permute-done.13 = bf16[2,4,128,512]{3,2,1,0:T(8,128)(2,1)} collective-permute-done((bf16[2,4,128,512]{3,2,1,0:T(8,128)(2,1)}, bf16[2,4,128,512]{3,2,1,0:T(8,128)(2,1)}, u32[]{:S(2)}, u32[]{:S(2)}) %collective-permute-start.13) | collective-permute-done | bytes 1048608 | tf_op jit(solution)/shard_map/ppermute | solution.py:456
  291.2 1.9 fusion.11
  293.1 1.6 collective-permute-start.14
  297.9 8.6 %collective-permute-done.14 = bf16[4,128,512]{2,1,0:T(8,128)(2,1)S(1)} collective-permute-done((bf16[4,128,512]{2,1,0:T(8,128)(2,1)S(1)}, bf16[4,128,512]{2,1,0:T(8,128)(2,1)S(1)}, u32[]{:S(2)}, u32[]{:S(2)}) %collective-permute-start.14) | collective-permute-done | bytes 524320 | tf_op jit(solution)/shard_map/ppermute | solution.py:456
  306.7 2.7 collective-permute-done.16
  312.4 2.1 fusion.42
  314.5 2.0 fusion.37
  316.5 2.1 add_convert_fusion.1
  325.3 2.7 collective-permute-done.9
  328.4 1.9 constant_dynamic-slice_fusion.1
  330.3 3.6 collective-permute-done.10
  335.9 2.0 multiply_reduce_fusion.3
  338.6 1.8 fusion.34
  340.4 3.6 all-to-all-start.1
  343.9 4.8 %fusion.22 = bf16[64,1024]{1,0:T(8,128)(2,1)} fusion(bf16[3072,1024]{1,0:T(8,128)(2,1)} %param.34, pred[64,3072]{1,0:T(32,128)(4,1)} %broadcast_in_dim.22, bf16[64,3072]{1,0:T(8,128)(2,1)S(1)} %squeeze.111, f32[1024]{0:T(1024)S(1)} %copy-done.30), kind=kOutput, calls=%fused_computation.50 | convolution fusion | flops 402980864 | bytes 7016448 | tf_op jit(solution)/shard_map/dot_general | solution.py:38
  349.6 3.0 collective-permute-start.12
  352.7 1.9 maximum_select_fusion.4
  354.5 5.4 %collective-permute-done.12 = f32[11,1024]{1,0:T(8,128)S(1)} collective-permute-done((f32[11,1024]{1,0:T(8,128)S(1)}, f32[11,1024]{1,0:T(8,128)S(1)}, u32[]{:S(2)}, u32[]{:S(2)}) %collective-permute-start.12) | collective-permute-done | bytes 45088 | tf_op jit(solution)/shard_map/ppermute | solution.py:497
  364.3 15.9 %reduce-scatter.11.cloned.1.call-done = bf16[1,2,128,512]{3,2,1,0:T(8,128)(2,1)} async-done(((bf16[4,2,128,512]{3,2,1,0:T(8,128)(2,1)}), bf16[1,2,128,512]{3,2,1,0:T(8,128)(2,1)}) %reduce-scatter.11.cloned.1.call-update) | async-done | bytes 262160 | tf_op jit(solution)/shard_map/reduce_scatter | solution.py:466
  384.4 66.9 %all-gather.8.cloned.1.call-done = bf16[3072,1024]{1,0:T(8,128)(2,1)} async-done(((bf16[96,1024]{1,0:T(8,128)(2,1)}), bf16[3072,1024]{1,0:T(8,128)(2,1)}) %all-gather.8.cloned.1.call-update) | async-done | bytes 6291472 | tf_op jit(solution)/shard_map/all_gather | solution.py:324
  451.3 9.1 %convert_element_type.259 = f32[3072,1024]{1,0:T(8,128)} convert(bf16[3072,1024]{1,0:T(8,128)(2,1)} %all-gather.8.cloned.1.call-done) | non-fusion elementwise | flops 3145728 | bytes 18874368 | tf_op jit(solution)/shard_map/convert_element_type | solution.py:324
  (247 shorter events, 60.8 us)
Async XLA Ops:
  8.0 4.3 copy-start
  8.1 4.1 copy-start.32
  11.6 2.8 collective-permute-start
  12.1 54.5 %collective-permute-start.1 = (f32[2,2]{0,1:T(2,128)S(1)}, f32[2,2]{0,1:T(2,128)S(1)}, u32[]{:S(2)}, u32[]{:S(2)}) collective-permute-start(f32[2,2]{0,1:T(2,128)S(1)} %add_convert_fusion.3), channel_id=1, source_target_pairs={{0,4},{4,0},{8,12},{12,8},{16,20},{20,16},{24,28},{28,24},{1,5},{5... | collective-permute-start | bytes 56 | tf_op jit(solution)/shard_map/ppermute | solution.py:279
  17.6 42.4 %copy-start.23 = (f32[1024]{0:T(1024)S(1)}, f32[1024]{0:T(1024)}, u32[]{:S(2)}) copy-start(f32[1024]{0:T(1024)} %param.24) | copy-start | bytes 12292
  17.6 42.4 %copy-start.25 = (f32[1024]{0:T(1024)S(1)}, f32[1024]{0:T(1024)}, u32[]{:S(2)}) copy-start(f32[1024]{0:T(1024)} %param.25) | copy-start | bytes 12292
  17.6 40.8 %all-to-all-start = ((bf16[4,176,1024]{2,1,0:T(8,128)(2,1)}), bf16[4,176,1024]{2,1,0:T(8,128)(2,1)S(1)}, u32[]{:S(2)}, u32[]{:S(2)}) async-start(bf16[4,176,1024]{2,1,0:T(8,128)(2,1)} %slice.194), calls=%async_computation | async-start | bytes 2883584 | tf_op jit(solution)/shard_map/all_to_all | solution.py:302
  23.9 89.6 %all-gather.6.cloned.1.call-start = ((), (), s32[]{:S(2)}) async-start(), calls=%async_computation.9 | async-start | bytes 2621440 | tf_op jit(solution)/shard_map/all_gather | solution.py:305
  58.4 38.6 %copy-start.2 = (bf16[4,176,1024]{2,1,0:T(8,128)(2,1)}, bf16[4,176,1024]{2,1,0:T(8,128)(2,1)S(1)}, u32[]{:S(2)}) copy-start(bf16[4,176,1024]{2,1,0:T(8,128)(2,1)S(1)} %all-to-all-done) | copy-start | bytes 4325380
  61.7 9.4 %collective-permute-start.2 = (bf16[704,1024]{1,0:T(8,128)(2,1)}, bf16[704,1024]{1,0:T(8,128)(2,1)}, u32[]{:S(2)}, u32[]{:S(2)}) collective-permute-start(bf16[704,1024]{1,0:T(8,128)(2,1)} %fusion.3), channel_id=1, source_target_pairs={{0,4},{4,0},{8,12},{12,8},{16,20},{20,16},{24,28},{28,24},{1,5},{5... | collective-permute-start | bytes 4325384 | tf_op jit(solution)/shard_map/ppermute | solution.py:279
  68.2 92.2 %all-gather.4.cloned.1.call-start = ((), (), s32[]{:S(2)}) async-start(), calls=%async_computation.8 | async-start | bytes 2621440 | tf_op jit(solution)/shard_map/all_gather | solution.py:371
  73.7 7.9 %copy-start.5 = (bf16[4,2,64,1024]{3,2,1,0:T(8,128)(2,1)}, bf16[4,2,64,1024]{3,2,1,0:T(8,128)(2,1)S(1)}, u32[]{:S(2)}) copy-start(bf16[4,2,64,1024]{3,2,1,0:T(8,128)(2,1)S(1)} %copy.108) | copy-start | bytes 3145732
  73.9 7.7 %copy-start.13 = (bf16[4,2,64,1024]{3,2,1,0:T(8,128)(2,1)}, bf16[4,2,64,1024]{3,2,1,0:T(8,128)(2,1)S(1)}, u32[]{:S(2)}) copy-start(bf16[4,2,64,1024]{3,2,1,0:T(8,128)(2,1)S(1)} %copy.109) | copy-start | bytes 3145732
  73.9 7.7 %copy-start.17 = (bf16[4,2,48,1024]{3,2,1,0:T(8,128)(2,1)}, bf16[4,2,48,1024]{3,2,1,0:T(8,128)(2,1)S(1)}, u32[]{:S(2)}) copy-start(bf16[4,2,48,1024]{3,2,1,0:T(8,128)(2,1)S(1)} %copy.110) | copy-start | bytes 2359300
  96.5 2.2 collective-permute-start.3
  106.6 118.7 %copy-start.26 = (f32[256]{0:T(256)}, f32[256]{0:T(256)S(1)}, u32[]{:S(2)}) copy-start(f32[256]{0:T(256)S(1)} %add_rsqrt_fusion.1) | copy-start | bytes 3076
  108.1 75.5 %reduce-scatter.15.cloned.1.call-start = ((), (), s32[]{:S(2)}) async-start(), calls=%async_computation.14 | async-start | bytes 7077888 | tf_op jit(solution)/shard_map/reduce_scatter | solution.py:322
  108.3 4.8 %copy-start.35 = (pred[2,96]{1,0:T(4,128)(4,1)}, pred[2,96]{1,0:T(4,128)(4,1)S(1)}, u32[]{:S(2)}) copy-start(pred[2,96]{1,0:T(4,128)(4,1)S(1)} %broadcast_compare_fusion) | copy-start | bytes 580
  113.1 112.2 %reduce-scatter.9.cloned.1.call-start = ((), (), s32[]{:S(2)}) async-start(), calls=%async_computation.11 | async-start | bytes 2621440 | tf_op jit(solution)/shard_map/reduce_scatter | solution.py:381
  183.5 127.2 %reduce-scatter.17.cloned.1.call-start = ((), (), s32[]{:S(2)}) async-start(), calls=%async_computation.15 | async-start | bytes 983040 | tf_op jit(solution)/shard_map/reduce_scatter | solution.py:323
  184.1 144.3 %reduce-scatter.7.cloned.1.call-start = ((), (), s32[]{:S(2)}) async-start(), calls=%async_computation.10 | async-start | bytes 2621440 | tf_op jit(solution)/shard_map/reduce_scatter | solution.py:380
  184.9 177.1 %reduce-scatter.13.cloned.1.call-start = ((), (), s32[]{:S(2)}) async-start(), calls=%async_computation.13 | async-start | bytes 4718592 | tf_op jit(solution)/shard_map/reduce_scatter | solution.py:376
  229.6 1.9 collective-permute-start.5
  230.9 149.3 %reduce-scatter.11.cloned.1.call-start = ((), (), s32[]{:S(2)}) async-start(), calls=%async_computation.12 | async-start | bytes 1310720 | tf_op jit(solution)/shard_map/reduce_scatter | solution.py:466
  265.5 25.7 %collective-permute-start.13 = (bf16[2,4,128,512]{3,2,1,0:T(8,128)(2,1)}, bf16[2,4,128,512]{3,2,1,0:T(8,128)(2,1)}, u32[]{:S(2)}, u32[]{:S(2)}) collective-permute-start(bf16[2,4,128,512]{3,2,1,0:T(8,128)(2,1)} %dynamic-slice_bitcast_fusion.1), channel_id=1, source_target_pairs={{0,8},{4,12},{8,0},{12,4},{16,24},{20,28},{24,16},{28,20},{1,9},{5... | collective-permute-start | bytes 3145736 | tf_op jit(solution)/shard_map/ppermute | solution.py:456
  268.2 26.5 %collective-permute-start.15 = (bf16[2,4,128,512]{3,2,1,0:T(8,128)(2,1)}, bf16[2,4,128,512]{3,2,1,0:T(8,128)(2,1)}, u32[]{:S(2)}, u32[]{:S(2)}) collective-permute-start(bf16[2,4,128,512]{3,2,1,0:T(8,128)(2,1)} %dynamic-slice_bitcast_fusion), channel_id=1, source_target_pairs={{0,16},{4,20},{8,24},{12,28},{16,0},{20,4},{24,8},{28,12},{1,17},{... | collective-permute-start | bytes 3145736 | tf_op jit(solution)/shard_map/ppermute | solution.py:456
  293.1 13.4 %collective-permute-start.14 = (bf16[4,128,512]{2,1,0:T(8,128)(2,1)S(1)}, bf16[4,128,512]{2,1,0:T(8,128)(2,1)S(1)}, u32[]{:S(2)}, u32[]{:S(2)}) collective-permute-start(bf16[4,128,512]{2,1,0:T(8,128)(2,1)S(1)} %dynamic-slice_bitcast_fusion.3), channel_id=1, source_target_pairs={{0,16},{4,20},{8,24},{12,28},{16,0},{20,4},{24,8},{28,12},{1,17},{... | collective-permute-start | bytes 1572872 | tf_op jit(solution)/shard_map/ppermute | solution.py:456
  296.3 13.1 %collective-permute-start.16 = (bf16[4,128,512]{2,1,0:T(8,128)(2,1)S(1)}, bf16[4,128,512]{2,1,0:T(8,128)(2,1)S(1)}, u32[]{:S(2)}, u32[]{:S(2)}) collective-permute-start(bf16[4,128,512]{2,1,0:T(8,128)(2,1)S(1)} %dynamic-slice_bitcast_fusion.2), channel_id=1, source_target_pairs={{0,8},{4,12},{8,0},{12,4},{16,24},{20,28},{24,16},{28,20},{1,9},{5... | collective-permute-start | bytes 1572872 | tf_op jit(solution)/shard_map/ppermute | solution.py:456
  306.6 4.7 copy-start.12
  306.6 4.8 %copy-start.31 = (f32[1,1024]{1,0:T(1,128)S(1)}, f32[1,1024]{1,0:T(1,128)}, u32[]{:S(2)}) copy-start(f32[1,1024]{1,0:T(1,128)} %get-tuple-element.33) | copy-start | bytes 12292
  306.6 5.1 %copy-start.22 = (f32[4,22,512]{2,1,0:T(8,128)S(1)}, f32[4,22,512]{2,1,0:T(8,128)}, u32[]{:S(2)}) copy-start(f32[4,22,512]{2,1,0:T(8,128)} %get-tuple-element.32) | copy-start | bytes 540676
  310.6 140.6 %all-gather.8.cloned.1.call-start = ((), (), s32[]{:S(2)}) async-start(), calls=%async_computation.16 | async-start | bytes 6488064 | tf_op jit(solution)/shard_map/all_gather | solution.py:324
  316.5 7.0 %copy-start.36 = (pred[2,96]{1,0:T(4,128)(4,1)S(1)}, pred[2,96]{1,0:T(4,128)(4,1)}, u32[]{:S(2)}) copy-start(pred[2,96]{1,0:T(4,128)(4,1)} %copy-done.35) | copy-start | bytes 580
  318.7 5.9 %copy-start.27 = (f32[4,176,1]{1,0,2:T(4,128)S(1)}, f32[4,176,1]{1,0,2:T(4,128)}, u32[]{:S(2)}) copy-start(f32[4,176,1]{1,0,2:T(4,128)} %get-tuple-element.161) | copy-start | bytes 8452
  319.7 15.4 %collective-permute-start.6 = (bf16[4,64,1024]{2,1,0:T(8,128)(2,1)S(1)}, bf16[4,64,1024]{2,1,0:T(8,128)(2,1)S(1)}, u32[]{:S(2)}, u32[]{:S(2)}) collective-permute-start(bf16[4,64,1024]{2,1,0:T(8,128)(2,1)S(1)} %dynamic-slice_bitcast_fusion.4), channel_id=1, source_target_pairs={{0,4},{4,0},{8,12},{12,8},{16,20},{20,16},{24,28},{28,24},{1,5},{5... | collective-permute-start | bytes 1572872 | tf_op jit(solution)/shard_map/ppermute | solution.py:279
  320.3 1.4 collective-permute-start.8
  321.8 6.2 %collective-permute-start.9 = (f32[11,1024]{1,0:T(8,128)S(1)}, f32[11,1024]{1,0:T(8,128)S(1)}, u32[]{:S(2)}, u32[]{:S(2)}) collective-permute-start(f32[11,1024]{1,0:T(8,128)S(1)} %add.297), channel_id=1, source_target_pairs={{0,8},{4,12},{8,0},{12,4},{16,24},{20,28},{24,16},{28,20},{1,9},{5... | collective-permute-start | bytes 135176 | tf_op jit(solution)/shard_map/ppermute | solution.py:495
  324.6 14.0 %copy-start.7 = (f32[256,1024]{1,0:T(8,128)S(1)}, f32[256,1024]{1,0:T(8,128)}, u32[]{:S(2)}) copy-start(f32[256,1024]{1,0:T(8,128)} %get-tuple-element.126) | copy-start | bytes 3145732
  328.0 5.9 %collective-permute-start.10 = (f32[11,1024]{1,0:T(8,128)S(1)}, f32[11,1024]{1,0:T(8,128)S(1)}, u32[]{:S(2)}, u32[]{:S(2)}) collective-permute-start(f32[11,1024]{1,0:T(8,128)S(1)} %add.298), channel_id=1, source_target_pairs={{0,16},{4,20},{8,24},{12,28},{16,0},{20,4},{24,8},{28,12},{1,17},{... | collective-permute-start | bytes 135176 | tf_op jit(solution)/shard_map/ppermute | solution.py:495
  330.3 22.4 %collective-permute-start.4 = (bf16[2,64,1024]{2,1,0:T(8,128)(2,1)}, bf16[2,64,1024]{2,1,0:T(8,128)(2,1)}, u32[]{:S(2)}, u32[]{:S(2)}) collective-permute-start(bf16[2,64,1024]{2,1,0:T(8,128)(2,1)} %get-tuple-element.144), channel_id=1, source_target_pairs={{0,4},{4,0},{8,12},{12,8},{16,20},{20,16},{24,28},{28,24},{1,5},{5... | collective-permute-start | bytes 786440 | tf_op jit(solution)/shard_map/ppermute | solution.py:279
  334.6 14.2 %collective-permute-start.11 = (f32[11,1024]{1,0:T(8,128)}, f32[11,1024]{1,0:T(8,128)}, u32[]{:S(2)}, u32[]{:S(2)}) collective-permute-start(f32[11,1024]{1,0:T(8,128)} %add.299), channel_id=1, source_target_pairs={{0,1},{1,0},{2,3},{3,2},{4,5},{5,4},{6,7},{7,6},{8,9},{9,8},{10,11... | collective-permute-start | bytes 135176 | tf_op jit(solution)/shard_map/ppermute | solution.py:497
  337.8 6.1 %copy-start.30 = (f32[1024]{0:T(1024)S(1)}, f32[1024]{0:T(1024)}, u32[]{:S(2)}) copy-start(f32[1024]{0:T(1024)} %param.35) | copy-start | bytes 12292
  340.4 19.6 %all-to-all-start.1 = ((bf16[4,64,1024]{2,1,0:T(8,128)(2,1)}), bf16[4,64,1024]{2,1,0:T(8,128)(2,1)S(1)}, u32[]{:S(2)}, u32[]{:S(2)}) async-start(bf16[4,64,1024]{2,1,0:T(8,128)(2,1)} %bitcast.279), calls=%async_computation.3 | async-start | bytes 1048576 | tf_op jit(solution)/shard_map/all_to_all | solution.py:423
  343.9 8.7 %copy-start.16 = (bf16[2,1,64,1024]{3,2,1,0:T(8,128)(2,1)S(1)}, bf16[2,1,64,1024]{3,2,1,0:T(8,128)(2,1)}, u32[]{:S(2)}) copy-start(bf16[2,1,64,1024]{3,2,1,0:T(8,128)(2,1)} %get-tuple-element.143) | copy-start | bytes 786436
  349.6 10.3 %collective-permute-start.12 = (f32[11,1024]{1,0:T(8,128)S(1)}, f32[11,1024]{1,0:T(8,128)S(1)}, u32[]{:S(2)}, u32[]{:S(2)}) collective-permute-start(f32[11,1024]{1,0:T(8,128)S(1)} %add.300), channel_id=1, source_target_pairs={{0,2},{1,3},{2,0},{3,1},{4,6},{5,7},{6,4},{7,5},{8,10},{9,11},{10,... | collective-permute-start | bytes 135176 | tf_op jit(solution)/shard_map/ppermute | solution.py:497
  360.0 3.2 collective-permute-start.7
  381.2 2.0 collective-permute-start.17
  451.3 9.1 %copy-start.1 = (f32[8,22]{1,0:T(8,128)S(1)}, f32[8,22]{1,0:T(8,128)}, u32[]{:S(2)}) copy-start(f32[8,22]{1,0:T(8,128)} %param.27) | copy-start | bytes 2116
  (19 other events, 45.8 us)
Sparse Core Ops, SparseCore 0:
  68.3 45.1 all-gather.5
  115.8 44.6 all-gather.3
Sparse Core Ops, SparseCore 1:
  113.2 60.7 reduce-scatter.14
  183.6 41.7 reduce-scatter.8
  227.5 22.2 reduce-scatter.16
  252.1 43.0 reduce-scatter.6
  298.9 51.8 reduce-scatter.12
  353.0 27.1 reduce-scatter.10
  383.4 67.9 all-gather.7
